TPU v7x, 32 devices: a whole 2x2x4 slice. The times are simulated.
32 devices in a mesh: img: 4 (over y, x), tpl: 8 (over z, core).
Axes of the slice: x: 2, y: 2, z: 4, core: 2. Of those that a mesh axis runs over, the one named last changes fastest.
Arguments:
- images: bfloat16 [6144, 2048], P(('img', 'tpl')), may hold values from -320 to 320
- templates: bfloat16 [3072, 2048], P('tpl'), may hold values from -0.62 to 0.62
- class_exponent: int32 [8], replicated, may hold values from 0 to 5
- class_mask: int32 [6144, 8], P('img'), may hold values from 0 to 1, as said below
Outputs:
- new_templates: float32 [3072, 2048], P('tpl', 'img')
- log_evidence: float32 [6144], P('img')
Inputs may be any that keep to these rules, and one draw needn't show every extreme that they name: `class_mask`: every image is compared with at least one class.
All inputs are finite; a program needn't handle non-finite values.
Results may differ from a plain program's by a relative error of at most 0.0023.
Values may be sent and summed in bfloat16 or wider, within the bound.
A program may use at most 64 MiB of HBM per device.

v0:
```python
import jax
import jax.numpy as jnp
from jax import lax
from jax.sharding import PartitionSpec as P

floor_score = -1e30


def per_device(images, templates, class_exponent, class_mask):
    tpl_rows = templates.shape[0]
    feature_count = templates.shape[1]
    class_count = class_exponent.shape[0]
    per_class = tpl_rows * lax.axis_size("tpl") // class_count
    global_rows = lax.axis_index("tpl") * tpl_rows + jnp.arange(tpl_rows, dtype=jnp.int32)
    owner = global_rows // per_class
    onehot = (jnp.arange(class_count, dtype=jnp.int32)[:, None] == owner[None, :]).astype(
        jnp.float32
    )
    inverse_temp = 0.5 * jnp.exp2(0.5 * class_exponent.astype(jnp.float32))
    template_beta = jnp.sum(onehot * inverse_temp[:, None], axis=0)
    allowed = jnp.dot(class_mask.astype(jnp.float32), onehot, precision=lax.Precision.HIGHEST) > 0.5
    squared_norm = jnp.sum(jnp.square(templates.astype(jnp.float32)), axis=1)
    gathered = lax.all_gather(images, "tpl", axis=0, tiled=True)
    raw = lax.dot_general(
        gathered, templates, (((1,), (1,)), ((), ())), preferred_element_type=jnp.float32
    )
    scores = template_beta[None, :] * (raw - 0.5 * squared_norm[None, :])
    local_top = jnp.max(jnp.where(allowed, scores, floor_score), axis=1)
    top = lax.pmax(local_top, "tpl")
    expo = jnp.where(allowed, jnp.exp(scores - top[:, None]), 0.0)
    totals = lax.psum(jnp.sum(expo, axis=1), "tpl")
    posterior = expo / totals[:, None]
    posterior_bf = posterior.astype(jnp.bfloat16)
    occupancy_part = jnp.sum(posterior, axis=0)
    weighted_part = lax.dot_general(
        posterior_bf, gathered, (((0,), (0,)), ((), ())), preferred_element_type=jnp.float32
    )
    columns = feature_count // lax.axis_size("img")
    col_start = lax.axis_index("img") * columns
    own_share = lax.psum_scatter(weighted_part, "img", scatter_dimension=1, tiled=True)
    occupancy = lax.psum(occupancy_part, "img")
    own_templates = lax.dynamic_slice_in_dim(templates, col_start, columns, 1).astype(jnp.float32)
    new_templates = (own_share + own_templates) / (occupancy[:, None] + 1.0)
    log_evidence = top + jnp.log(totals)
    return (new_templates, log_evidence)


def solution(mesh):
    in_specs = (P(("img", "tpl"), None), P("tpl", None), P(), P("img", None))
    out_specs = (P("tpl", "img"), P("img"))
    return jax.shard_map(
        per_device, mesh=mesh, in_specs=in_specs, out_specs=out_specs, check_vma=False
    )
```

profile of v0, /device:TPU:0, one launch (start us, length us, event | category | flops | bytes accessed | tf_op | source)
XLA Modules:
  0.0 171.4 jit_solution(5243481778394577077)
XLA Ops:
  7.2 0.0 all-gather.2.cloned.1.call-start
  7.2 0.7 all-gather.2.cloned.1.call-update
  7.9 0.0 reduce-scatter.2.cloned.1.call-start
  8.0 0.7 exponential_multiply_fusion
  8.6 0.1 select_reduce_fusion.1
  8.7 1.8 %multiply_reduce_fusion = f32[384]{0:T(512)S(1)} fusion(bf16[384,2048]{1,0:T(8,128)(2,1)} %param.5), kind=kLoop, calls=%fused_computation | loop fusion | flops 2358912 | bytes 1574400 | tf_op jit(solution)/shard_map/reduce_sum | solution.py:22
  10.5 0.0 copy-start
  10.5 66.5 %all-gather.2.cloned.1.call-done = bf16[1536,2048]{1,0:T(8,128)(2,1)} async-done(((bf16[192,2048]{1,0:T(8,128)(2,1)}), bf16[1536,2048]{1,0:T(8,128)(2,1)}) %all-gather.2.cloned.1.call-update) | async-done | bytes 6291472 | tf_op jit(solution)/shard_map/all_gather | solution.py:23
  77.1 5.2 %fusion = f32[1536,384]{0,1:T(8,128)S(1)} fusion(bf16[1536,2048]{1,0:T(8,128)(2,1)} %all-gather.2.cloned.1.call-done, bf16[384,2048]{1,0:T(8,128)(2,1)} %param.5, f32[384]{0:T(512)S(1)} %broadcast_multiply_fusion, f32[384]{0:T(512)S(1)} %select_reduce_fusion.1), kind=kOutput, calls=%fused_computation.2 | convolution fusion | flops 2417098752 | bytes 10226688 | tf_op jit(solution)/shard_map/dot_general | solution.py:24
  82.3 0.0 copy-done
  82.3 1.5 select_reduce_fusion
  83.8 14.4 %pmax.7 = f32[1536]{0:T(1024)S(1)} all-reduce(f32[1536]{0:T(1024)S(1)} %get-tuple-element.2), channel_id=1, replica_groups=mesh['img'=4,'tpl'=8] {'tpl'}, use_global_device_ids=true, to_apply=%region_3.4 | all-reduce | flops 1536 | bytes 12288 | tf_op jit(solution)/shard_map/pmax | solution.py:29
  98.3 0.6 fusion.3
  98.8 13.9 %psum.14 = f32[1536]{0:T(1024)S(1)} all-reduce(f32[1536]{0:T(1024)S(1)} %fusion.3), channel_id=1, replica_groups=mesh['img'=4,'tpl'=8] {'tpl'}, use_global_device_ids=true, to_apply=%region_5.6 | all-reduce | flops 1536 | bytes 12288 | tf_op jit(solution)/shard_map/psum | solution.py:31
  112.8 7.1 %fusion.4 = f32[384,2048]{1,0:T(8,128)} fusion(bf16[1536,2048]{1,0:T(8,128)(2,1)} %all-gather.2.cloned.1.call-done, pred[1536,384]{0,1:T(32,128)(4,1)S(1)} %get-tuple-element.3, f32[1536,384]{0,1:T(8,128)S(1)} %fusion, f32[1536]{0:T(1024)S(1)} %psum.14, f32[1536]{0:T(1024)S(1)} %pmax.7), kind=kOutput, calls=%fused_computation.9 | convolution fusion | flops 2418278400 | bytes 12398592 | tf_op jit(solution)/shard_map/dot_general | solution.py:35
  119.9 0.0 reduce-scatter.2.cloned.1.call-update
  119.9 0.7 fusion.6
  120.6 10.4 %psum.15 = f32[384]{0:T(512)S(1)} all-reduce(f32[384]{0:T(512)S(1)} %fusion.6), channel_id=1, replica_groups=mesh['img'=4,'tpl'=8] {'img'}, use_global_device_ids=true, to_apply=%region_8.9 | all-reduce | flops 384 | bytes 3072 | tf_op jit(solution)/shard_map/psum | solution.py:41
  131.0 0.6 log_add_fusion
  131.6 30.7 %reduce-scatter.2.cloned.1.call-done = f32[384,512]{1,0:T(8,128)} async-done(((f32[384,2048]{1,0:T(8,128)}), f32[384,512]{1,0:T(8,128)}) %reduce-scatter.2.cloned.1.call-update) | async-done | bytes 786448 | tf_op jit(solution)/shard_map/reduce_scatter | solution.py:40
  162.3 2.2 %add_divide_fusion = f32[384,512]{1,0:T(8,128)} fusion(f32[384,512]{1,0:T(8,128)} %reduce-scatter.2.cloned.1.call-done, f32[384]{0:T(512)S(1)} %broadcast_add_fusion, bf16[384,2048]{1,0:T(8,128)(2,1)} %param.5, s32[]{:T(128)S(6)} %select_n.22), kind=kLoop, calls=%fused_computation.11 | loop fusion | flops 589824 | bytes 1967620 | tf_op jit(solution)/shard_map/div | solution.py:43
  (3 shorter events, 0.0 us)
Async XLA Ops:
  7.2 69.9 %all-gather.2.cloned.1.call-start = ((), (), s32[]{:S(2)}) async-start(), calls=%async_computation.1 | async-start | bytes 7077888 | tf_op jit(solution)/shard_map/all_gather | solution.py:23
  7.9 154.4 %reduce-scatter.2.cloned.1.call-start = ((), (), s32[]{:S(2)}) async-start(), calls=%async_computation.2 | async-start | bytes 3932160 | tf_op jit(solution)/shard_map/reduce_scatter | solution.py:40
  10.5 71.8 %copy-start = (s32[1536,8]{0,1:T(8,128)S(1)}, s32[1536,8]{0,1:T(8,128)}, u32[]{:S(2)}) copy-start(s32[1536,8]{0,1:T(8,128)} %param.7) | copy-start | bytes 147460
Sparse Core Ops, SparseCore 0:
  9.6 67.4 all-gather.1
  120.0 42.2 reduce-scatter.1
where the time goes:
time: 172 us; the launch traced here: 171 us
  waiting for transfers between devices  97.9 us (57%)
  blocking collectives  38.7 us (23%)
  between operations  14.1 us (8%)
  matrix products  13.9 us (8%)
  other arithmetic  6.69 us (4%)
    all_gather x1, waiting for transfers between devices, per_device(): gathered = lax.all_gather(images, 'tpl', axis=0, tiled=True)  66.5 us
    reduce_scatter x1, waiting for transfers between devices, per_device(): lax.psum_scatter(weighted_part, 'img', scatter_dimension=1, tiled=True)  30.7 us
    pmax x1, blocking collectives, per_device(): top = lax.pmax(local_top, 'tpl')  14.4 us
    psum x1, blocking collectives, per_device(): totals = lax.psum(jnp.sum(expo, axis=1), 'tpl')  13.9 us
    psum x1, blocking collectives, per_device(): occupancy = lax.psum(occupancy_part, 'img')  10.4 us
    dot_general x1, matrix products, per_device(): lax.dot_general(posterior_bf, gathered, (((0,), (0,)), ((), ())), preferr...  7.11 us
    dot_general x1, matrix products, per_device(): lax.dot_general(gathered, templates, (((1,), (1,)), ((), ())), preferred_...  5.24 us
  transfers between devices with their start and end apart: 2, of which 2 were waited for; matrix products, arithmetic and copies ran while one was open for 2% of the time, Pallas kernels for 0%

commit v1 on v0

--- a/solution.py
+++ b/solution.py
@@ -1,9 +1,27 @@
+import functools
 import jax
 import jax.numpy as jnp
 from jax import lax
 from jax.sharding import PartitionSpec as P
+from jax.lax import axis_index, axis_size, ppermute
 
 floor_score = -1e30
+
+
+def change_patch_now(message, net_axis):
+    cores_n = axis_size(net_axis)
+    left_arr = [(i0 - 1, i0) for i0 in range(1, cores_n)] + [(cores_n - 1, 0)]
+    response = message
+    found = [response]
+    for _ in tuple(range(cores_n - 1)):
+        response = ppermute(response, net_axis, left_arr)
+        found += [response]
+    far_arr = jnp.concatenate([*reversed(found)], 0)
+    t1 = jnp.roll(far_arr, (axis_index(net_axis) + 1) * response.shape[0], 0)
+    return t1
+
+
+_find_case = functools.partial(change_patch_now, net_axis="tpl")
 
 
 def per_device(images, templates, class_exponent, class_mask):
@@ -20,7 +38,7 @@
     template_beta = jnp.sum(onehot * inverse_temp[:, None], axis=0)
     allowed = jnp.dot(class_mask.astype(jnp.float32), onehot, precision=lax.Precision.HIGHEST) > 0.5
     squared_norm = jnp.sum(jnp.square(templates.astype(jnp.float32)), axis=1)
-    gathered = lax.all_gather(images, "tpl", axis=0, tiled=True)
+    gathered = _find_case(images)
     raw = lax.dot_general(
         gathered, templates, (((1,), (1,)), ((), ())), preferred_element_type=jnp.float32
     )

time: 172 us -> 205 us (1.19)
  waiting for transfers between devices: 97.9 us -> 122 us
  local copies, waits for them, and re-layouts: 0.01 us -> 10.4 us
  matrix products: 13.9 us -> 11.7 us
    ppermute x0 -> x7, waiting for transfers between devices: none -> 91.6 us  [change_patch_now(): response = ppermute(response, net_axis, left_arr)]
    all_gather x1 -> x0, waiting for transfers between devices: 66.5 us -> none  [per_device(): gathered = lax.all_gather(images, 'tpl', axis=0, tiled=True)]
    unnamed x2 -> x23, local copies, waits for them, and re-layouts: 0.01 us -> 10.4 us
    dot_general x1, matrix products: 5.24 us -> 2.66 us  [per_device(): lax.dot_general(gathered, templates, (((1,), (1,)), ((), ())), preferred_...]
  transfers between devices with their start and end apart: 2 -> 8, of which waited for: 2 -> 8; matrix products, arithmetic and copies ran while one was open for 2% -> 2% of each run, Pallas kernels for 0% -> 0%
where the time goes in v1:
time: 205 us
  waiting for transfers between devices  122 us (60%)
  blocking collectives  38.5 us (19%)
  between operations  14.3 us (7%)
  matrix products  11.7 us (6%)
  local copies, waits for them, and re-layouts  10.4 us (5%)
  other arithmetic  6.67 us (3%)
    ppermute x7, waiting for transfers between devices, change_patch_now(): response = ppermute(response, net_axis, left_arr)  91.6 us
    reduce_scatter x1, waiting for transfers between devices, per_device(): lax.psum_scatter(weighted_part, 'img', scatter_dimension=1, tiled=True)  30.7 us
    psum x1, blocking collectives, per_device(): totals = lax.psum(jnp.sum(expo, axis=1), 'tpl')  13.9 us
    pmax x1, blocking collectives, per_device(): top = lax.pmax(local_top, 'tpl')  13.9 us
    psum x1, blocking collectives, per_device(): occupancy = lax.psum(occupancy_part, 'img')  10.7 us
    unnamed x23, local copies, waits for them, and re-layouts  10.4 us
    dot_general x1, matrix products, per_device(): lax.dot_general(posterior_bf, gathered, (((0,), (0,)), ((), ())), preferr...  7.47 us
  transfers between devices with their start and end apart: 8, of which 8 were waited for; matrix products, arithmetic and copies ran while one was open for 2% of the time, Pallas kernels for 0%

profile of v1, /device:TPU:0, one launch (start us, length us, event | category | flops | bytes accessed | tf_op | source)
XLA Modules:
  0.0 204.5 jit_solution(11704750248180981720)
XLA Ops:
  7.2 0.0 reduce-scatter.2.cloned.1.call-start
  7.2 0.5 collective-permute-start
  7.8 13.9 %collective-permute-done = bf16[192,2048]{1,0:T(8,128)(2,1)S(1)} collective-permute-done((bf16[192,2048]{1,0:T(8,128)(2,1)}, bf16[192,2048]{1,0:T(8,128)(2,1)S(1)}, u32[]{:S(2)}, u32[]{:S(2)}) %collective-permute-start) | collective-permute-done | bytes 786464 | tf_op jit(solution)/shard_map/ppermute | solution.py:17
  21.7 0.0 collective-permute-start.1
  21.7 13.2 %collective-permute-done.1 = bf16[192,2048]{1,0:T(8,128)(2,1)S(1)} collective-permute-done((bf16[192,2048]{1,0:T(8,128)(2,1)S(1)}, bf16[192,2048]{1,0:T(8,128)(2,1)S(1)}, u32[]{:S(2)}, u32[]{:S(2)}) %collective-permute-start.1) | collective-permute-done | bytes 786464 | tf_op jit(solution)/shard_map/ppermute | solution.py:17
  34.9 0.0 collective-permute-start.2
  34.9 13.2 %collective-permute-done.2 = bf16[192,2048]{1,0:T(8,128)(2,1)S(1)} collective-permute-done((bf16[192,2048]{1,0:T(8,128)(2,1)S(1)}, bf16[192,2048]{1,0:T(8,128)(2,1)S(1)}, u32[]{:S(2)}, u32[]{:S(2)}) %collective-permute-start.2) | collective-permute-done | bytes 786464 | tf_op jit(solution)/shard_map/ppermute | solution.py:17
  48.1 0.0 collective-permute-start.3
  48.1 13.3 %collective-permute-done.3 = bf16[192,2048]{1,0:T(8,128)(2,1)} collective-permute-done((bf16[192,2048]{1,0:T(8,128)(2,1)S(1)}, bf16[192,2048]{1,0:T(8,128)(2,1)}, u32[]{:S(2)}, u32[]{:S(2)}) %collective-permute-start.3) | collective-permute-done | bytes 786464 | tf_op jit(solution)/shard_map/ppermute | solution.py:17
  61.4 0.0 collective-permute-start.4
  61.4 13.5 %collective-permute-done.4 = bf16[192,2048]{1,0:T(8,128)(2,1)} collective-permute-done((bf16[192,2048]{1,0:T(8,128)(2,1)}, bf16[192,2048]{1,0:T(8,128)(2,1)}, u32[]{:S(2)}, u32[]{:S(2)}) %collective-permute-start.4) | collective-permute-done | bytes 786464 | tf_op jit(solution)/shard_map/ppermute | solution.py:17
  74.9 0.0 collective-permute-start.5
  75.0 13.5 %collective-permute-done.5 = bf16[192,2048]{1,0:T(8,128)(2,1)} collective-permute-done((bf16[192,2048]{1,0:T(8,128)(2,1)}, bf16[192,2048]{1,0:T(8,128)(2,1)}, u32[]{:S(2)}, u32[]{:S(2)}) %collective-permute-start.5) | collective-permute-done | bytes 786464 | tf_op jit(solution)/shard_map/ppermute | solution.py:17
  88.5 0.0 collective-permute-start.6
  88.5 0.7 exponential_multiply_fusion
  89.2 0.1 select_reduce_fusion.1
  89.3 1.8 multiply_reduce_fusion
  91.1 10.9 %collective-permute-done.6 = bf16[192,2048]{1,0:T(8,128)(2,1)} collective-permute-done((bf16[192,2048]{1,0:T(8,128)(2,1)}, bf16[192,2048]{1,0:T(8,128)(2,1)}, u32[]{:S(2)}, u32[]{:S(2)}) %collective-permute-start.6) | collective-permute-done | bytes 786464 | tf_op jit(solution)/shard_map/ppermute | solution.py:17
  102.0 1.2 constant_dynamic-update-slice_fusion.15
  103.2 1.2 constant_dynamic-update-slice_fusion.14
  104.4 1.2 constant_dynamic-update-slice_fusion.13
  105.6 1.2 constant_dynamic-update-slice_fusion.12
  106.8 0.1 constant_dynamic-update-slice_fusion.11
  106.9 0.1 constant_dynamic-update-slice_fusion.10
  107.0 0.1 constant_dynamic-update-slice_fusion.9
  107.0 0.1 constant_dynamic-update-slice_fusion.8
  107.1 1.2 constant_dynamic-update-slice_fusion.7
  108.3 1.2 constant_dynamic-update-slice_fusion.6
  109.5 1.2 constant_dynamic-update-slice_fusion.5
  110.7 0.0 copy-start.3
  110.7 1.2 constant_dynamic-update-slice_fusion.4
  112.0 0.1 constant_dynamic-update-slice_fusion.3
  112.0 0.1 constant_dynamic-update-slice_fusion.2
  112.1 0.1 constant_dynamic-update-slice_fusion.1
  112.1 0.1 constant_dynamic-update-slice_fusion
  112.2 2.7 %fusion.7 = f32[1536,384]{0,1:T(8,128)S(1)} fusion(bf16[384,2048]{1,0:T(8,128)(2,1)S(1)} %copy-done.1, bf16[3072,2048]{1,0:T(8,128)(2,1)S(1)} %constant_dynamic-update-slice_fusion, s32[]{:T(128)S(6)} %select_n.34, f32[384]{0:T(512)S(1)} %broadcast_multiply_fusion, f32[384]{0:T(512)S(1)} %select_reduce_fusion.1), kind=kOutput, calls=%fused_computation.6 | convolution fusion | flops 2417098752 | bytes 10227716 | tf_op jit(solution)/shard_map/dot_general | solution.py:42
  114.9 1.5 select_reduce_fusion
  116.4 0.4 copy-done.2
  116.8 13.9 %pmax.7 = f32[1536]{0:T(1024)S(1)} all-reduce(f32[1536]{0:T(1024)S(1)} %get-tuple-element.2), channel_id=1, replica_groups=mesh['img'=4,'tpl'=8] {'tpl'}, use_global_device_ids=true, to_apply=%region_3.4 | all-reduce | flops 1536 | bytes 12288 | tf_op jit(solution)/shard_map/pmax | solution.py:47
  130.7 0.6 fusion.12
  131.2 13.9 %psum.14 = f32[1536]{0:T(1024)S(1)} all-reduce(f32[1536]{0:T(1024)S(1)} %fusion.12), channel_id=1, replica_groups=mesh['img'=4,'tpl'=8] {'tpl'}, use_global_device_ids=true, to_apply=%region_5.6 | all-reduce | flops 1536 | bytes 12288 | tf_op jit(solution)/shard_map/psum | solution.py:49
  145.2 7.5 %fusion = f32[384,2048]{1,0:T(8,128)} fusion(bf16[3072,2048]{1,0:T(8,128)(2,1)} %copy-done.2, s32[]{:T(128)S(6)} %select_n.34, pred[1536,384]{0,1:T(32,128)(4,1)S(1)} %get-tuple-element.3, f32[1536,384]{0,1:T(8,128)S(1)} %fusion.7, f32[1536]{0:T(1024)S(1)} %psum.14, f32[1536]{0:T(1024)S(1)} %pmax.7), kind=kOutput, calls=%fused_computation | convolution fusion | flops 2418278400 | bytes 12398596 | tf_op jit(solution)/shard_map/dot_general | solution.py:53
  152.6 0.0 reduce-scatter.2.cloned.1.call-update
  152.7 0.7 fusion.14
  153.4 10.7 %psum.15 = f32[384]{0:T(512)S(1)} all-reduce(f32[384]{0:T(512)S(1)} %fusion.14), channel_id=1, replica_groups=mesh['img'=4,'tpl'=8] {'img'}, use_global_device_ids=true, to_apply=%region_8.9 | all-reduce | flops 384 | bytes 3072 | tf_op jit(solution)/shard_map/psum | solution.py:59
  164.1 0.6 log_add_fusion
  164.7 30.7 %reduce-scatter.2.cloned.1.call-done = f32[384,512]{1,0:T(8,128)} async-done(((f32[384,2048]{1,0:T(8,128)}), f32[384,512]{1,0:T(8,128)}) %reduce-scatter.2.cloned.1.call-update) | async-done | bytes 786448 | tf_op jit(solution)/shard_map/reduce_scatter | solution.py:58
  195.4 2.2 %add_divide_fusion = f32[384,512]{1,0:T(8,128)} fusion(f32[384,512]{1,0:T(8,128)} %reduce-scatter.2.cloned.1.call-done, f32[384]{0:T(512)S(1)} %broadcast_add_fusion, bf16[384,2048]{1,0:T(8,128)(2,1)} %param.5, s32[]{:T(128)S(6)} %select_n.37), kind=kLoop, calls=%fused_computation.14 | loop fusion | flops 589824 | bytes 1967620 | tf_op jit(solution)/shard_map/div | solution.py:61
  (9 shorter events, 0.0 us)
Async XLA Ops:
  7.2 99.9 %copy-start = (bf16[192,2048]{1,0:T(8,128)(2,1)S(1)}, bf16[192,2048]{1,0:T(8,128)(2,1)}, u32[]{:S(2)}) copy-start(bf16[192,2048]{1,0:T(8,128)(2,1)} %param.4) | copy-start | bytes 2359300
  7.2 188.3 %reduce-scatter.2.cloned.1.call-start = ((), (), s32[]{:S(2)}) async-start(), calls=%async_computation.1 | async-start | bytes 3932160 | tf_op jit(solution)/shard_map/reduce_scatter | solution.py:58
  7.2 14.5 %collective-permute-start = (bf16[192,2048]{1,0:T(8,128)(2,1)}, bf16[192,2048]{1,0:T(8,128)(2,1)S(1)}, u32[]{:S(2)}, u32[]{:S(2)}) collective-permute-start(bf16[192,2048]{1,0:T(8,128)(2,1)} %param.4), channel_id=1, source_target_pairs={{0,1},{1,2},{2,3},{3,4},{4,5},{5,6},{6,7},{7,0},{8,9},{9,10},{10,1... | collective-permute-start | bytes 2359304 | tf_op jit(solution)/shard_map/ppermute | solution.py:17
  21.7 13.2 %collective-permute-start.1 = (bf16[192,2048]{1,0:T(8,128)(2,1)S(1)}, bf16[192,2048]{1,0:T(8,128)(2,1)S(1)}, u32[]{:S(2)}, u32[]{:S(2)}) collective-permute-start(bf16[192,2048]{1,0:T(8,128)(2,1)S(1)} %collective-permute-done), channel_id=1, source_target_pairs={{0,1},{1,2},{2,3},{3,4},{4,5},{5,6},{6,7},{7,0},{8,9},{9,10},{10,1... | collective-permute-start | bytes 2359304 | tf_op jit(solution)/shard_map/ppermute | solution.py:17
  34.9 13.2 %collective-permute-start.2 = (bf16[192,2048]{1,0:T(8,128)(2,1)S(1)}, bf16[192,2048]{1,0:T(8,128)(2,1)S(1)}, u32[]{:S(2)}, u32[]{:S(2)}) collective-permute-start(bf16[192,2048]{1,0:T(8,128)(2,1)S(1)} %collective-permute-done.1), channel_id=1, source_target_pairs={{0,1},{1,2},{2,3},{3,4},{4,5},{5,6},{6,7},{7,0},{8,9},{9,10},{10,1... | collective-permute-start | bytes 2359304 | tf_op jit(solution)/shard_map/ppermute | solution.py:17
  48.1 13.3 %collective-permute-start.3 = (bf16[192,2048]{1,0:T(8,128)(2,1)S(1)}, bf16[192,2048]{1,0:T(8,128)(2,1)}, u32[]{:S(2)}, u32[]{:S(2)}) collective-permute-start(bf16[192,2048]{1,0:T(8,128)(2,1)S(1)} %collective-permute-done.2), channel_id=1, source_target_pairs={{0,1},{1,2},{2,3},{3,4},{4,5},{5,6},{6,7},{7,0},{8,9},{9,10},{10,1... | collective-permute-start | bytes 2359304 | tf_op jit(solution)/shard_map/ppermute | solution.py:17
  61.4 13.5 %collective-permute-start.4 = (bf16[192,2048]{1,0:T(8,128)(2,1)}, bf16[192,2048]{1,0:T(8,128)(2,1)}, u32[]{:S(2)}, u32[]{:S(2)}) collective-permute-start(bf16[192,2048]{1,0:T(8,128)(2,1)} %collective-permute-done.3), channel_id=1, source_target_pairs={{0,1},{1,2},{2,3},{3,4},{4,5},{5,6},{6,7},{7,0},{8,9},{9,10},{10,1... | collective-permute-start | bytes 2359304 | tf_op jit(solution)/shard_map/ppermute | solution.py:17
  74.9 13.5 %collective-permute-start.5 = (bf16[192,2048]{1,0:T(8,128)(2,1)}, bf16[192,2048]{1,0:T(8,128)(2,1)}, u32[]{:S(2)}, u32[]{:S(2)}) collective-permute-start(bf16[192,2048]{1,0:T(8,128)(2,1)} %collective-permute-done.4), channel_id=1, source_target_pairs={{0,1},{1,2},{2,3},{3,4},{4,5},{5,6},{6,7},{7,0},{8,9},{9,10},{10,1... | collective-permute-start | bytes 2359304 | tf_op jit(solution)/shard_map/ppermute | solution.py:17
  88.5 13.5 %collective-permute-start.6 = (bf16[192,2048]{1,0:T(8,128)(2,1)}, bf16[192,2048]{1,0:T(8,128)(2,1)}, u32[]{:S(2)}, u32[]{:S(2)}) collective-permute-start(bf16[192,2048]{1,0:T(8,128)(2,1)} %collective-permute-done.5), channel_id=1, source_target_pairs={{0,1},{1,2},{2,3},{3,4},{4,5},{5,6},{6,7},{7,0},{8,9},{9,10},{10,1... | collective-permute-start | bytes 2359304 | tf_op jit(solution)/shard_map/ppermute | solution.py:17
  91.1 21.1 %copy-start.1 = (bf16[384,2048]{1,0:T(8,128)(2,1)S(1)}, bf16[384,2048]{1,0:T(8,128)(2,1)}, u32[]{:S(2)}) copy-start(bf16[384,2048]{1,0:T(8,128)(2,1)} %param.5) | copy-start | bytes 4718596
  110.7 4.2 %copy-start.3 = (s32[1536,8]{0,1:T(8,128)S(1)}, s32[1536,8]{0,1:T(8,128)}, u32[]{:S(2)}) copy-start(s32[1536,8]{0,1:T(8,128)} %param.7) | copy-start | bytes 147460
  112.2 4.6 %copy-start.2 = (bf16[3072,2048]{1,0:T(8,128)(2,1)}, bf16[3072,2048]{1,0:T(8,128)(2,1)S(1)}, u32[]{:S(2)}) copy-start(bf16[3072,2048]{1,0:T(8,128)(2,1)S(1)} %constant_dynamic-update-slice_fusion) | copy-start | bytes 37748740
Sparse Core Ops, SparseCore 0:
  152.8 42.6 reduce-scatter.1
